TPU v7x, 32 devices: a whole 2x2x4 slice. The times are simulated.
32 devices in a mesh: heads: 16 (over z, y, core), width: 2 (over x).
Axes of the slice: x: 2, y: 2, z: 4, core: 2. Of those that a mesh axis runs over, the one named last changes fastest.
Arguments:
- out_grad: bfloat16 [512, 7168], P('heads', 'width'), may hold values from -24 to 24
- w_out: float32 [4096, 7168], P('heads', 'width'), may hold values from -0.09375 to 0.09375
- row_moment: float32 [4096], P('heads'), may hold values from 4 to 400
- col_moment: float32 [7168], P('width'), may hold values from 4 to 400
- queries: bfloat16 [512, 6144], P('width', 'heads'), may hold values from -240 to 240
- latent: bfloat16 [512, 512], P('width'), may hold values from -6 to 6
- key_rope: bfloat16 [512, 64], P('width'), may hold values from -4 to 4
- w_kv_up: bfloat16 [512, 8192], P(None, 'heads'), may hold values from -0.25 to 0.25
- doc_lengths: int32 [2, 4], P('width'), may hold values from 1 to 160, 256 in all within a row
Outputs:
- weight_update: float32 [4096, 7168], P('heads', 'width')
- query_grad: bfloat16 [512, 6144], P('width', 'heads')
- latent_grad: float32 [512, 576], P('width', 'heads')
- kv_up_grad: float32 [512, 8192], P('width', 'heads')
Inputs may be any that keep to these rules, and one draw needn't show every extreme that they name: `doc_lengths`: row p holds the lengths of the 4 documents packed in order into pack p; they sum to 256 and the longest in every row is exactly 160.
All inputs are finite; a program needn't handle non-finite values.
Results may differ from a plain program's by a relative error of at most 0.0088.
Values may be sent and summed in bfloat16 or wider, within the bound.
No kernel may reach another device: no remote copies, remote signals or barrier semaphores. Data moves between devices by JAX's collectives and lax.ppermute only.
A program may use at most 64 MiB of HBM per device.

v0:
```python
import jax
import jax.numpy as jnp
from jax import lax
from jax.sharding import PartitionSpec as P

D = 7168
VD = 128
NOPE = 128
ROPE = 64


moment_decay = 0.9
update_eps = 1e-06


def doc_mask(lengths, length):
    doc_ends = jnp.cumsum(lengths)
    position = jnp.arange(length, dtype=jnp.int32)
    document = jnp.sum((position[:, None] >= doc_ends[None, :]).astype(jnp.int32), axis=1)
    return (document[:, None] == document[None, :]) & (position[None, :] <= position[:, None])


def forward_pack(queries, latent, key_rope, w_kv_up, allowed):
    length = queries.shape[0]
    n_heads = w_kv_up.shape[1] // (NOPE + VD)
    scale_factor = (NOPE + ROPE) ** (-0.5)
    key_value = jnp.dot(latent, w_kv_up, preferred_element_type=jnp.float32).astype(jnp.bfloat16)
    key_value = key_value.reshape(length, n_heads, NOPE + VD)
    key_nope = key_value[:, :, :NOPE]
    values = key_value[:, :, NOPE:]
    query_heads = queries.reshape(length, n_heads, NOPE + ROPE)
    scores = jnp.einsum(
        "ihd,jhd->hij", query_heads[:, :, :NOPE], key_nope, preferred_element_type=jnp.float32
    )
    scores = scores + jnp.einsum(
        "ihd,jd->hij", query_heads[:, :, NOPE:], key_rope, preferred_element_type=jnp.float32
    )
    scores = scores * scale_factor
    masked = jnp.where(allowed[None], scores, -jnp.inf)
    highest = jnp.max(masked, axis=2, keepdims=True)
    weights = jnp.exp(masked - highest)
    prob_full = weights / jnp.sum(weights, axis=2, keepdims=True)
    probs_half = prob_full.astype(jnp.bfloat16)
    attended = jnp.einsum("hij,jhd->ihd", probs_half, values, preferred_element_type=jnp.float32)
    attended = attended.astype(jnp.bfloat16).reshape(length, n_heads * VD)
    return (query_heads, key_nope, values, prob_full, probs_half, attended)


def backward_pack(states, attn_half, key_rope, w_kv_up):
    query_heads, key_nope, values, prob_full, probs_half, attended = states
    length = query_heads.shape[0]
    n_heads = query_heads.shape[1]
    scale_factor = (NOPE + ROPE) ** (-0.5)
    grad_heads = attn_half.reshape(length, n_heads, VD)
    row_delta = jnp.sum(
        grad_heads.astype(jnp.float32) * attended.reshape(length, n_heads, VD).astype(jnp.float32),
        axis=2,
    ).T
    prob_grad = jnp.einsum("ihd,jhd->hij", grad_heads, values, preferred_element_type=jnp.float32)
    score_grad = (prob_full * (prob_grad - row_delta[:, :, None]) * scale_factor).astype(
        jnp.bfloat16
    )
    nope_grad = jnp.einsum("hij,jhd->ihd", score_grad, key_nope, preferred_element_type=jnp.float32)
    rotary_grad = jnp.einsum(
        "hij,jd->ihd", score_grad, key_rope, preferred_element_type=jnp.float32
    )
    query_grad = jnp.concatenate([nope_grad, rotary_grad], axis=2).astype(jnp.bfloat16)
    query_grad = query_grad.reshape(length, n_heads * (NOPE + ROPE))
    key_nope_grad = jnp.einsum(
        "hij,ihd->jhd", score_grad, query_heads[:, :, :NOPE], preferred_element_type=jnp.float32
    )
    rope_grad = jnp.einsum(
        "hij,ihd->jd", score_grad, query_heads[:, :, NOPE:], preferred_element_type=jnp.float32
    )
    value_grad = jnp.einsum(
        "hij,ihd->jhd", probs_half, grad_heads, preferred_element_type=jnp.float32
    )
    kv_grad = jnp.concatenate([key_nope_grad, value_grad], axis=2).astype(jnp.bfloat16)
    kv_grad = kv_grad.reshape(length, n_heads * (NOPE + VD))
    latent_part = lax.dot_general(
        kv_grad, w_kv_up, (((1,), (1,)), ((), ())), preferred_element_type=jnp.float32
    )
    latent_term = jnp.concatenate([latent_part, rope_grad], axis=1)
    return (query_grad, latent_term, kv_grad)


def on_device(
    out_grad, w_out, row_moment, col_moment, queries, latent, key_rope, w_kv_up, doc_lengths
):
    length = queries.shape[0]
    allowed = doc_mask(doc_lengths[0], length)
    states = forward_pack(queries, latent, key_rope, w_kv_up, allowed)
    attended = states[5]
    w_half = w_out.astype(jnp.bfloat16)
    grad_rows = lax.all_gather(out_grad, "heads", axis=0, tiled=True)
    picked = grad_rows
    attn_grad = lax.psum_scatter(
        lax.dot_general(
            picked, w_half, (((1,), (1,)), ((), ())), preferred_element_type=jnp.float32
        ),
        "width",
        scatter_dimension=0,
        tiled=True,
    )
    attn_half = attn_grad.astype(jnp.bfloat16)
    picked = grad_rows
    gradient = lax.dot_general(
        lax.all_gather(attended, "width", axis=0, tiled=True),
        picked,
        (((0,), (0,)), ((), ())),
        preferred_element_type=jnp.float32,
    )
    query_grad, latent_term, kv_grad = backward_pack(states, attn_half, key_rope, w_kv_up)
    latent_grad = lax.psum_scatter(latent_term, "heads", scatter_dimension=1, tiled=True)
    picked = latent
    kv_up_grad = lax.psum_scatter(
        lax.dot_general(
            picked, kv_grad, (((0,), (0,)), ((), ())), preferred_element_type=jnp.float32
        ),
        "width",
        scatter_dimension=0,
        tiled=True,
    )
    squares = gradient * gradient
    row_part = jnp.sum(squares, axis=1)
    col_part = jnp.sum(squares, axis=0)
    row_count = gradient.shape[0]
    col_count = gradient.shape[1]
    rows_total = row_count * lax.axis_size("heads")
    head_index = lax.axis_index("heads")
    width_index = lax.axis_index("width")
    row_full = lax.dynamic_update_slice(
        jnp.zeros((rows_total,), jnp.float32), row_part, (head_index * row_count,)
    )
    col_full = lax.dynamic_update_slice(
        jnp.zeros((D,), jnp.float32), col_part, (width_index * col_count,)
    )
    row_all, col_all = lax.psum((row_full, col_full), ("heads", "width"))
    row_sum = lax.dynamic_slice_in_dim(row_all, head_index * row_count, row_count, 0)
    col_sum = lax.dynamic_slice_in_dim(col_all, width_index * col_count, col_count, 0)
    row_new = moment_decay * row_moment + (1.0 - moment_decay) * row_sum / D
    col_new = moment_decay * col_moment + (1.0 - moment_decay) * col_sum / rows_total
    scaled = gradient / jnp.sqrt(row_new[:, None] * col_new[None, :])
    mean_square = lax.psum(jnp.sum(scaled * scaled), ("heads", "width")) / (rows_total * D)
    weight_update = scaled / jnp.sqrt(mean_square + update_eps)
    return (weight_update, query_grad, latent_grad, kv_up_grad)


def solution(mesh):
    in_specs = (
        P("heads", "width"),
        P("heads", "width"),
        P("heads"),
        P("width"),
        P("width", "heads"),
        P("width", None),
        P("width", None),
        P(None, "heads"),
        P("width", None),
    )
    out_specs = (P("heads", "width"), P("width", "heads"), P("width", "heads"), P("width", "heads"))
    return jax.shard_map(
        on_device, mesh=mesh, in_specs=in_specs, out_specs=out_specs, check_vma=False
    )
```

profile of v0, /device:TPU:0, one launch (start us, length us, event | category | flops | bytes accessed | tf_op | source)
XLA Modules:
  0.0 205.8 jit_solution(9484889876110462075)
XLA Ops:
  7.2 0.0 copy-start
  7.2 0.0 all-gather.2.cloned.1.call-start
  7.2 0.7 all-gather.2.cloned.1.call-update
  7.9 0.0 reduce-scatter.4.cloned.1.call-start
  8.0 1.1 copy.75
  9.0 0.0 copy-done
  9.0 1.2 convolution_convert_fusion
  10.3 0.1 reshape.95
  10.4 0.2 fusion.28
  10.6 0.1 copy.108
  10.7 0.8 reduce-window.8
  11.5 1.2 dynamic-slice
  12.8 0.0 copy-start.2
  12.8 47.9 %all-gather.2.cloned.1.call-done = bf16[512,3584]{1,0:T(8,128)(2,1)} async-done(((bf16[32,3584]{1,0:T(8,128)(2,1)}), bf16[512,3584]{1,0:T(8,128)(2,1)}) %all-gather.2.cloned.1.call-update) | async-done | bytes 3670032 | tf_op jit(solution)/shard_map/all_gather | solution.py:95
  60.7 5.1 %fusion.2 = f32[512,256]{1,0:T(8,128)} fusion(bf16[512,3584]{1,0:T(8,128)(2,1)} %all-gather.2.cloned.1.call-done, f32[256,3584]{1,0:T(8,128)} %param.10), kind=kOutput, calls=%fused_computation.6 | convolution fusion | flops 940441600 | bytes 7864320 | tf_op jit(solution)/shard_map/dot_general | solution.py:98
  65.8 0.0 reduce-scatter.4.cloned.1.call-update
  65.8 0.0 all-reduce.4.cloned.1.call-start
  65.8 0.1 convert_reduce_fusion
  65.9 0.1 fusion.16
  66.0 0.2 convolution_bitcast_fusion.2
  66.3 0.0 copy-done.2
  66.3 0.3 fusion.10
  66.5 0.4 fusion.29
  66.9 12.4 %reduce-scatter.4.cloned.1.call-done = f32[256,256]{1,0:T(8,128)} async-done(((f32[512,256]{1,0:T(8,128)}), f32[256,256]{1,0:T(8,128)}) %reduce-scatter.4.cloned.1.call-update) | async-done | bytes 262160 | tf_op jit(solution)/shard_map/reduce_scatter | solution.py:97
  79.3 1.0 convert_element_type.46
  80.3 0.1 copy.78
  80.4 0.3 multiply_reduce_fusion.3
  80.7 0.3 fusion.14
  81.0 0.3 fusion.11
  81.2 0.2 fusion.13
  81.5 0.2 convolution_bitcast_fusion.3
  81.7 0.3 fusion.30
  82.1 0.9 pad_maximum_fusion
  82.9 0.0 all-reduce.4.cloned.1.call-update
  83.0 0.0 reduce-scatter.6.cloned.1.call-start
  83.0 5.7 %all_gather.6 = bf16[512,256]{0,1:T(8,128)(2,1)S(1)} all-gather(bf16[256,256]{0,1:T(8,128)(2,1)S(1)} %bitcast.69), channel_id=1, replica_groups=mesh['heads'=16,'width'=2] {'width'}, dimensions={0}, use_global_device_ids=true | all-gather | bytes 393216 | tf_op jit(solution)/shard_map/all_gather | solution.py:108
  88.8 0.0 copy-start.3
  88.8 0.0 copy-start.4
  88.8 0.0 copy-start.1
  88.8 5.1 %multiply_reduce_fusion.2 = (f32[256]{0:T(256)S(1)}, f32[3584]{0:T(1024)S(1)}, f32[256,3584]{1,0:T(8,128)}) fusion(bf16[512,256]{0,1:T(8,128)(2,1)S(1)} %all_gather.6, bf16[512,3584]{1,0:T(8,128)(2,1)} %all-gather.2.cloned.1.call-done), kind=kOutput, calls=%fused_computation.4 | convolution fusion | flops 942272768 | bytes 7617536 | tf_op jit(solution)/shard_map/dot_general | solution.py:107
  93.8 0.3 dynamic_update_slice.7
  94.2 0.3 dynamic_update_slice.6
  94.5 40.0 %all-reduce.1 = (f32[7168]{0:T(1024)S(1)}, f32[4096]{0:T(1024)S(1)}) all-reduce(f32[7168]{0:T(1024)S(1)} %dynamic_update_slice.7, f32[4096]{0:T(1024)S(1)} %dynamic_update_slice.6), channel_id=1, replica_groups=mesh['heads'=16,'width'=2] {'heads','width'}, use_global_device_ids=true, to_apply=%region_7.8 | all-reduce | flops 11264 | bytes 90112 | tf_op jit(solution)/shard_map/psum | solution.py:138
  134.5 0.0 copy-done.3
  134.5 0.1 multiply_add_fusion
  134.6 0.0 copy-done.4
  134.6 0.1 multiply_add_fusion.1
  134.6 0.0 copy-done.1
  134.6 1.3 convolution_bitcast_fusion
  135.9 0.0 reduce-scatter.6.cloned.1.call-update
  136.0 3.7 %multiply_reduce_fusion = f32[]{:T(128)} fusion(f32[256,3584]{1,0:T(8,128)} %get-tuple-element.28, f32[3584]{0:T(1024)S(1)} %multiply_add_fusion, f32[256]{0:T(256)S(1)} %multiply_add_fusion.1), kind=kLoop, calls=%fused_computation.1 | loop fusion | flops 3670015 | bytes 3685380 | tf_op jit(solution)/shard_map/reduce_sum | solution.py:144
  140.3 41.3 %psum.23 = f32[]{:T(128)} all-reduce(f32[]{:T(128)} %multiply_reduce_fusion), channel_id=1, replica_groups=mesh['heads'=16,'width'=2] {'heads','width'}, use_global_device_ids=true, to_apply=%region_9.10 | all-reduce | flops 1 | bytes 8 | tf_op jit(solution)/shard_map/psum | solution.py:144
  181.5 0.2 fusion.15
  181.7 0.2 fusion.12
  182.0 0.8 copy.90
  183.5 4.4 %fusion.1 = f32[256,3584]{1,0:T(8,128)} fusion(f32[256,3584]{1,0:T(8,128)} %get-tuple-element.28, f32[]{:T(128)S(6)} %sqrt.7, f32[3584]{0:T(1024)S(1)} %multiply_add_fusion, f32[256]{0:T(256)S(1)} %multiply_add_fusion.1), kind=kLoop, calls=%fused_computation.5 | loop fusion | flops 2752512 | bytes 7355396 | tf_op jit(solution)/shard_map/div | solution.py:145
  187.9 0.0 all-reduce.4.cloned.1.call-done
  187.9 1.0 constant_dynamic-slice_fusion
  189.0 0.7 copy.91
  189.7 7.6 %reduce-scatter.6.cloned.1.call-done = f32[256,512]{0,1:T(8,128)} async-done(((f32[512,512]{0,1:T(8,128)}), f32[256,512]{0,1:T(8,128)}) %reduce-scatter.6.cloned.1.call-update) | async-done | bytes 524304 | tf_op jit(solution)/shard_map/reduce_scatter | solution.py:116
  197.2 2.0 copy.92
  (4 shorter events, 0.0 us)
Async XLA Ops:
  7.2 1.9 copy-start
  7.2 53.5 %all-gather.2.cloned.1.call-start = ((), (), s32[]{:S(2)}) async-start(), calls=%async_computation.2 | async-start | bytes 3899392 | tf_op jit(solution)/shard_map/all_gather | solution.py:95
  7.9 71.4 %reduce-scatter.4.cloned.1.call-start = ((), (), s32[]{:S(2)}) async-start(), calls=%async_computation.3 | async-start | bytes 786432 | tf_op jit(solution)/shard_map/reduce_scatter | solution.py:97
  12.8 53.5 %copy-start.2 = (bf16[256,64]{0,1:T(8,128)(2,1)S(1)}, bf16[256,64]{0,1:T(8,128)(2,1)}, u32[]{:S(2)}) copy-start(bf16[256,64]{0,1:T(8,128)(2,1)} %param.15) | copy-start | bytes 98308
  65.8 122.1 %all-reduce.4.cloned.1.call-start = ((), (), s32[]{:S(2)}) async-start(), calls=%async_computation.5 | async-start | bytes 1310720
  83.0 114.3 %reduce-scatter.6.cloned.1.call-start = ((), (), s32[]{:S(2)}) async-start(), calls=%async_computation.4 | async-start | bytes 1572864 | tf_op jit(solution)/shard_map/reduce_scatter | solution.py:116
  88.8 45.7 %copy-start.3 = (f32[3584]{0:T(1024)S(1)}, f32[3584]{0:T(1024)}, u32[]{:S(2)}) copy-start(f32[3584]{0:T(1024)} %param.12) | copy-start | bytes 43012
  88.8 45.8 %copy-start.4 = (f32[256]{0:T(256)S(1)}, f32[256]{0:T(256)}, u32[]{:S(2)}) copy-start(f32[256]{0:T(256)} %param.11) | copy-start | bytes 3076
  88.8 45.9 %copy-start.1 = (bf16[256,512]{1,0:T(8,128)(2,1)S(1)}, bf16[256,512]{1,0:T(8,128)(2,1)}, u32[]{:S(2)}) copy-start(bf16[256,512]{1,0:T(8,128)(2,1)} %param.14) | copy-start | bytes 786436
Sparse Core Ops, SparseCore 0:
  10.3 50.3 all-gather.1
  65.9 13.3 reduce-scatter.3
  83.1 91.8 all-reduce.3
  177.1 20.1 reduce-scatter.5
where the time goes:
time: 206 us
  blocking collectives  87 us (42%)
  waiting for transfers between devices  68.6 us (33%)
  between operations  15.3 us (7%)
  matrix products  15.2 us (7%)
  other arithmetic  11.6 us (6%)
  local copies, waits for them, and re-layouts  8.01 us (4%)
    all_gather x1, waiting for transfers between devices, on_device(): grad_rows = lax.all_gather(out_grad, 'heads', axis=0, tiled=True)  47.9 us
    psum x1, blocking collectives, on_device(): lax.psum(jnp.sum(scaled * scaled), ('heads', 'width')) / (rows_total * D)  41.3 us
    psum x1, blocking collectives, on_device(): row_all, col_all = lax.psum((row_full, col_full), ('heads', 'width'))  40 us
    reduce_scatter x1, waiting for transfers between devices, on_device(): lax.psum_scatter(lax.dot_general(picked, w_half, (((1,), (1,)), ((), ()))...  12.4 us
    reduce_scatter x1, waiting for transfers between devices, on_device(): lax.psum_scatter(lax.dot_general(picked, kv_grad, (((0,), (0,)), ((), ())...  7.56 us
    unnamed x17, local copies, waits for them, and re-layouts  7.03 us
    all_gather x1, blocking collectives, on_device(): lax.all_gather(attended, 'width', axis=0, tiled=True)  5.74 us
    dot_general x1, matrix products, on_device(): lax.dot_general(picked, w_half, (((1,), (1,)), ((), ())), preferred_eleme...  5.1 us
  transfers between devices with their start and end apart: 4, of which 3 were waited for; matrix products, arithmetic and copies ran while one was open for 12% of the time, Pallas kernels for 0%

commit v1 on v0

--- a/solution.py
+++ b/solution.py
@@ -11,6 +11,56 @@
 
 moment_decay = 0.9
 update_eps = 1e-06
+
+
+def xor_swap(x, axis, bit):
+    size = lax.axis_size(axis)
+    return lax.ppermute(x, axis, [(i, i ^ bit) for i in range(size)])
+
+
+def bits_down(size):
+    bits = []
+    bit = size // 2
+    while bit:
+        bits.append(bit)
+        bit //= 2
+    return bits
+
+
+def gather_xor(x, axis):
+    size = lax.axis_size(axis)
+    parts = {0: x}
+    for bit in bits_down(size):
+        for mask in list(parts):
+            parts[mask | bit] = xor_swap(parts[mask], axis, bit)
+    return [parts[mask] for mask in range(size)]
+
+
+def reduce_scatter_xor(x, axis):
+    size = lax.axis_size(axis)
+    index = lax.axis_index(axis)
+    bit = 1
+    while bit < size:
+        pairs = x.reshape((x.shape[0] // 2, 2) + x.shape[1:])
+        own = (index // bit) % 2
+        keep = lax.dynamic_index_in_dim(pairs, own, 1, keepdims=False)
+        give = lax.dynamic_index_in_dim(pairs, 1 - own, 1, keepdims=False)
+        x = keep + xor_swap(give.astype(jnp.bfloat16), axis, bit).astype(jnp.float32)
+        bit *= 2
+    return x[0]
+
+
+def all_sum_xor(x, axis):
+    bit = 1
+    while bit < lax.axis_size(axis):
+        x = x + xor_swap(x, axis, bit)
+        bit *= 2
+    return x
+
+
+def scatter_sum_xor(x, axis):
+    size = lax.axis_size(axis)
+    return reduce_scatter_xor(x.reshape((size, x.shape[0] // size) + x.shape[1:]), axis)
 
 
 def doc_mask(lengths, length):
@@ -70,7 +120,7 @@
         "hij,ihd->jhd", score_grad, query_heads[:, :, :NOPE], preferred_element_type=jnp.float32
     )
     rope_grad = jnp.einsum(
-        "hij,ihd->jd", score_grad, query_heads[:, :, NOPE:], preferred_element_type=jnp.float32
+        "hij,ihd->dj", score_grad, query_heads[:, :, NOPE:], preferred_element_type=jnp.float32
     )
     value_grad = jnp.einsum(
         "hij,ihd->jhd", probs_half, grad_heads, preferred_element_type=jnp.float32
@@ -78,9 +128,9 @@
     kv_grad = jnp.concatenate([key_nope_grad, value_grad], axis=2).astype(jnp.bfloat16)
     kv_grad = kv_grad.reshape(length, n_heads * (NOPE + VD))
     latent_part = lax.dot_general(
-        kv_grad, w_kv_up, (((1,), (1,)), ((), ())), preferred_element_type=jnp.float32
-    )
-    latent_term = jnp.concatenate([latent_part, rope_grad], axis=1)
+        w_kv_up, kv_grad, (((1,), (1,)), ((), ())), preferred_element_type=jnp.float32
+    )
+    latent_term = jnp.concatenate([latent_part, rope_grad], axis=0)
     return (query_grad, latent_term, kv_grad)
 
 
@@ -88,61 +138,57 @@
     out_grad, w_out, row_moment, col_moment, queries, latent, key_rope, w_kv_up, doc_lengths
 ):
     length = queries.shape[0]
+    head_count = lax.axis_size("heads")
+    head_index = lax.axis_index("heads")
+    width_count = lax.axis_size("width")
+    width_index = lax.axis_index("width")
+    tokens = length * width_count
+    parts = gather_xor(out_grad, "heads")
+    grad_rows = jnp.concatenate(parts, axis=0)
+    order = head_index ^ jnp.arange(head_count, dtype=jnp.int32)
+
     allowed = doc_mask(doc_lengths[0], length)
     states = forward_pack(queries, latent, key_rope, w_kv_up, allowed)
     attended = states[5]
+    attended_parts = gather_xor(attended, "width")
+    order_width = width_index ^ jnp.arange(width_count, dtype=jnp.int32)
+    attended_all = jnp.stack(attended_parts)[order_width].reshape(
+        head_count, tokens // head_count, attended.shape[1]
+    )
     w_half = w_out.astype(jnp.bfloat16)
-    grad_rows = lax.all_gather(out_grad, "heads", axis=0, tiled=True)
-    picked = grad_rows
-    attn_grad = lax.psum_scatter(
+    attn_part = lax.dot_general(
+        grad_rows, w_half, (((1,), (1,)), ((), ())), preferred_element_type=jnp.float32
+    )
+    attn_part = attn_part.reshape(head_count, tokens // head_count, -1)[order]
+    attn_grad = scatter_sum_xor(attn_part.reshape(tokens, -1), "width")
+    attn_half = attn_grad.astype(jnp.bfloat16)
+    gradient = lax.dot_general(
+        attended_all[order].reshape(tokens, -1),
+        grad_rows,
+        (((0,), (0,)), ((), ())),
+        preferred_element_type=jnp.float32,
+    )
+    query_grad, latent_term, kv_grad = backward_pack(states, attn_half, key_rope, w_kv_up)
+    latent_grad = scatter_sum_xor(latent_term, "heads").T
+    kv_up_grad = scatter_sum_xor(
         lax.dot_general(
-            picked, w_half, (((1,), (1,)), ((), ())), preferred_element_type=jnp.float32
+            latent, kv_grad, (((0,), (0,)), ((), ())), preferred_element_type=jnp.float32
         ),
         "width",
-        scatter_dimension=0,
-        tiled=True,
-    )
-    attn_half = attn_grad.astype(jnp.bfloat16)
-    picked = grad_rows
-    gradient = lax.dot_general(
-        lax.all_gather(attended, "width", axis=0, tiled=True),
-        picked,
-        (((0,), (0,)), ((), ())),
-        preferred_element_type=jnp.float32,
-    )
-    query_grad, latent_term, kv_grad = backward_pack(states, attn_half, key_rope, w_kv_up)
-    latent_grad = lax.psum_scatter(latent_term, "heads", scatter_dimension=1, tiled=True)
-    picked = latent
-    kv_up_grad = lax.psum_scatter(
-        lax.dot_general(
-            picked, kv_grad, (((0,), (0,)), ((), ())), preferred_element_type=jnp.float32
-        ),
-        "width",
-        scatter_dimension=0,
-        tiled=True,
     )
     squares = gradient * gradient
-    row_part = jnp.sum(squares, axis=1)
-    col_part = jnp.sum(squares, axis=0)
-    row_count = gradient.shape[0]
-    col_count = gradient.shape[1]
-    rows_total = row_count * lax.axis_size("heads")
-    head_index = lax.axis_index("heads")
-    width_index = lax.axis_index("width")
-    row_full = lax.dynamic_update_slice(
-        jnp.zeros((rows_total,), jnp.float32), row_part, (head_index * row_count,)
-    )
-    col_full = lax.dynamic_update_slice(
-        jnp.zeros((D,), jnp.float32), col_part, (width_index * col_count,)
-    )
-    row_all, col_all = lax.psum((row_full, col_full), ("heads", "width"))
-    row_sum = lax.dynamic_slice_in_dim(row_all, head_index * row_count, row_count, 0)
-    col_sum = lax.dynamic_slice_in_dim(col_all, width_index * col_count, col_count, 0)
+    rows_total = gradient.shape[0] * head_count
+    row_sum = all_sum_xor(jnp.sum(squares, axis=1), "width")
     row_new = moment_decay * row_moment + (1.0 - moment_decay) * row_sum / D
-    col_new = moment_decay * col_moment + (1.0 - moment_decay) * col_sum / rows_total
-    scaled = gradient / jnp.sqrt(row_new[:, None] * col_new[None, :])
-    mean_square = lax.psum(jnp.sum(scaled * scaled), ("heads", "width")) / (rows_total * D)
-    weight_update = scaled / jnp.sqrt(mean_square + update_eps)
+    col_pair = jnp.stack(
+        [jnp.sum(squares, axis=0), jnp.sum(squares * (1.0 / row_new)[:, None], axis=0)]
+    )
+    col_pair = all_sum_xor(col_pair, "heads")
+    col_new = moment_decay * col_moment + (1.0 - moment_decay) * col_pair[0] / rows_total
+    mean_square = all_sum_xor(jnp.sum(col_pair[1] / col_new), "width") / (rows_total * D)
+    row_factor = lax.rsqrt(row_new)
+    col_factor = lax.rsqrt(col_new) * lax.rsqrt(mean_square + update_eps)
+    weight_update = gradient * row_factor[:, None] * col_factor[None, :]
     return (weight_update, query_grad, latent_grad, kv_up_grad)
 
 

time: 206 us -> 112 us (0.54)
  blocking collectives: 87 us -> 0 us
  waiting for transfers between devices: 68.6 us -> 40.9 us
  starting transfers between devices: 0.16 us -> 23.2 us
  between operations: 15.3 us -> 2.54 us
  local copies, waits for them, and re-layouts: 8.01 us -> 19.3 us
  matrix products: 15.2 us -> 12.2 us
    psum x2 -> x0, blocking collectives: 81.3 us -> none  [the longest x1 41.3 us: on_device(): lax.psum(jnp.sum(scaled * scaled), ('heads', 'width')) / (rows_total * D)]
    all_gather x1 -> x0, waiting for transfers between devices: 47.9 us -> none  [on_device(): grad_rows = lax.all_gather(out_grad, 'heads', axis=0, tiled=True)]
    ppermute x0 -> x28, waiting for transfers between devices: none -> 40.9 us  [xor_swap(): return lax.ppermute(x, axis, [(i, i ^ bit) for i in range(size)])]
    ppermute x0 -> x28, starting transfers between devices: none -> 23.2 us  [xor_swap(): return lax.ppermute(x, axis, [(i, i ^ bit) for i in range(size)])]
    reduce_scatter x2 -> x0, waiting for transfers between devices: 19.9 us -> none  [the longest x1 12.4 us: on_device(): lax.psum_scatter(lax.dot_general(picked, w_half, (((1,), (1,)), ((), ()))...]
    unnamed x17 -> x36, local copies, waits for them, and re-layouts: 7.03 us -> 14.3 us
    all_gather x1 -> x0, blocking collectives: 5.74 us -> none  [on_device(): lax.all_gather(attended, 'width', axis=0, tiled=True)]
    mul x0 -> x2, other arithmetic: none -> 4.39 us  [the longest x1 4.38 us: on_device(): weight_update = gradient * row_factor[:, None] * col_factor[None, :]]
  transfers between devices with their start and end apart: 4 -> 28, of which waited for: 3 -> 13; matrix products, arithmetic and copies ran while one was open for 12% -> 32% of each run, Pallas kernels for 0% -> 0%
where the time goes in v1:
time: 112 us; the launch traced here: 111 us
  waiting for transfers between devices  40.9 us (37%)
  starting transfers between devices  23.2 us (21%)
  local copies, waits for them, and re-layouts  19.3 us (17%)
  other arithmetic  12.9 us (12%)
  matrix products  12.2 us (11%)
  between operations  2.54 us (2%)
    ppermute x28, waiting for transfers between devices, xor_swap(): return lax.ppermute(x, axis, [(i, i ^ bit) for i in range(size)])  40.9 us
    ppermute x28, starting transfers between devices, xor_swap(): return lax.ppermute(x, axis, [(i, i ^ bit) for i in range(size)])  23.2 us
    unnamed x36, local copies, waits for them, and re-layouts  14.3 us
    dot_general x1, matrix products, on_device(): lax.dot_general(attended_all[order].reshape(tokens, -1), grad_rows, (((0,...  4.97 us
    mul x1, other arithmetic, on_device(): weight_update = gradient * row_factor[:, None] * col_factor[None, :]  4.38 us
    dot_general x1, matrix products, on_device(): lax.dot_general(grad_rows, w_half, (((1,), (1,)), ((), ())), preferred_el...  3.18 us
    reduce_sum x1, other arithmetic, on_device(): jnp.sum(squares, axis=0)  2.62 us
  transfers between devices with their start and end apart: 28, of which 13 were waited for; matrix products, arithmetic and copies ran while one was open for 32% of the time, Pallas kernels for 0%

profile of v1, /device:TPU:0, one launch (start us, length us, event | category | flops | bytes accessed | tf_op | source)
XLA Modules:
  0.0 111.2 jit_solution(17250228001673578010)
XLA Ops:
  0.7 3.1 %collective-permute-start.2 = (bf16[32,3584]{1,0:T(8,128)(2,1)}, bf16[32,3584]{1,0:T(8,128)(2,1)S(1)}, u32[]{:S(2)}, u32[]{:S(2)}) collective-permute-start(bf16[32,3584]{1,0:T(8,128)(2,1)} %param.9), channel_id=1, source_target_pairs={{0,4},{2,6},{4,0},{6,2},{8,12},{10,14},{12,8},{14,10},{16,20},{18,... | collective-permute-start | bytes 688136 | tf_op jit(solution)/shard_map/ppermute | solution.py:18
  3.7 1.6 %collective-permute-start.4 = (bf16[32,3584]{1,0:T(8,128)(2,1)}, bf16[32,3584]{1,0:T(8,128)(2,1)S(1)}, u32[]{:S(2)}, u32[]{:S(2)}) collective-permute-start(bf16[32,3584]{1,0:T(8,128)(2,1)} %param.9), channel_id=1, source_target_pairs={{0,8},{2,10},{4,12},{6,14},{8,0},{10,2},{12,4},{14,6},{16,24},{18,... | collective-permute-start | bytes 688136 | tf_op jit(solution)/shard_map/ppermute | solution.py:18
  5.3 2.6 %collective-permute-start.8 = (bf16[32,3584]{1,0:T(8,128)(2,1)}, bf16[32,3584]{1,0:T(8,128)(2,1)S(1)}, u32[]{:S(2)}, u32[]{:S(2)}) collective-permute-start(bf16[32,3584]{1,0:T(8,128)(2,1)} %param.9), channel_id=1, source_target_pairs={{0,16},{2,18},{4,20},{6,22},{8,24},{10,26},{12,28},{14,30},{16,0},... | collective-permute-start | bytes 688136 | tf_op jit(solution)/shard_map/ppermute | solution.py:18
  7.9 1.7 %constant_dynamic-update-slice_fusion.15 = bf16[512,3584]{1,0:T(8,128)(2,1)} fusion(bf16[32,3584]{1,0:T(8,128)(2,1)} %param.9), kind=kLoop, calls=%fused_computation.83 | loop fusion | bytes 458752
  9.6 1.1 copy.101
  10.7 1.2 %convolution_convert_fusion = bf16[256,512]{1,0:T(8,128)(2,1)S(1)} fusion(bf16[256,512]{1,0:T(8,128)(2,1)} %param.14, bf16[512,512]{1,0:T(8,128)(2,1)S(1)} %copy-done), kind=kOutput, calls=%fused_computation.22 | convolution fusion | flops 134348800 | bytes 1048576 | tf_op jit(solution)/shard_map/dot_general | solution.py:77
  12.2 0.8 reduce-window.8
  13.7 0.4 fusion.39
  14.1 2.6 %collective-permute-done.4 = bf16[32,3584]{1,0:T(8,128)(2,1)S(1)} collective-permute-done((bf16[32,3584]{1,0:T(8,128)(2,1)}, bf16[32,3584]{1,0:T(8,128)(2,1)S(1)}, u32[]{:S(2)}, u32[]{:S(2)}) %collective-permute-start.4) | collective-permute-done | bytes 229408 | tf_op jit(solution)/shard_map/ppermute | solution.py:18
  17.1 2.0 %collective-permute-done.8 = bf16[32,3584]{1,0:T(8,128)(2,1)S(1)} collective-permute-done((bf16[32,3584]{1,0:T(8,128)(2,1)}, bf16[32,3584]{1,0:T(8,128)(2,1)S(1)}, u32[]{:S(2)}, u32[]{:S(2)}) %collective-permute-start.8) | collective-permute-done | bytes 229408 | tf_op jit(solution)/shard_map/ppermute | solution.py:18
  19.1 0.4 collective-permute-start.12
  19.8 0.7 constant_dynamic-update-slice_fusion.14
  20.5 0.7 constant_dynamic-update-slice_fusion.13
  21.2 0.5 collective-permute-start.10
  21.7 5.4 %collective-permute-done.12 = bf16[32,3584]{1,0:T(8,128)(2,1)S(1)} collective-permute-done((bf16[32,3584]{1,0:T(8,128)(2,1)S(1)}, bf16[32,3584]{1,0:T(8,128)(2,1)S(1)}, u32[]{:S(2)}, u32[]{:S(2)}) %collective-permute-start.12) | collective-permute-done | bytes 229408 | tf_op jit(solution)/shard_map/ppermute | solution.py:18
  27.1 0.7 constant_dynamic-update-slice_fusion.12
  27.9 0.7 constant_dynamic-update-slice_fusion.11
  28.6 0.5 collective-permute-start.14
  29.7 0.7 constant_dynamic-update-slice_fusion.10
  30.4 0.7 constant_dynamic-update-slice_fusion.9
  31.1 5.5 %collective-permute-done.14 = bf16[32,3584]{1,0:T(8,128)(2,1)S(1)} collective-permute-done((bf16[32,3584]{1,0:T(8,128)(2,1)S(1)}, bf16[32,3584]{1,0:T(8,128)(2,1)S(1)}, u32[]{:S(2)}, u32[]{:S(2)}) %collective-permute-start.14) | collective-permute-done | bytes 229408 | tf_op jit(solution)/shard_map/ppermute | solution.py:18
  36.6 0.7 constant_dynamic-update-slice_fusion.8
  37.3 0.7 constant_dynamic-update-slice_fusion.7
  38.0 0.7 constant_dynamic-update-slice_fusion.6
  38.7 0.7 constant_dynamic-update-slice_fusion.5
  39.4 0.7 constant_dynamic-update-slice_fusion.4
  40.1 0.7 constant_dynamic-update-slice_fusion.3
  40.8 0.7 constant_dynamic-update-slice_fusion.2
  41.5 0.7 constant_dynamic-update-slice_fusion.1
  42.2 0.7 constant_dynamic-update-slice_fusion
  42.9 3.2 %fusion.1 = f32[512,256]{1,0:T(8,128)S(1)} fusion(bf16[512,3584]{1,0:T(8,128)(2,1)} %constant_dynamic-update-slice_fusion, f32[256,3584]{1,0:T(8,128)S(1)} %copy-done.1), kind=kOutput, calls=%fused_computation.8 | convolution fusion | flops 940441600 | bytes 7864320 | tf_op jit(solution)/shard_map/dot_general | solution.py:159
  46.1 0.6 gather_fusion.2
  46.7 1.6 %collective-permute-start.22 = (bf16[1,256,256]{2,1,0:T(8,128)(2,1)S(1)}, bf16[1,256,256]{2,1,0:T(8,128)(2,1)S(1)}, u32[]{:S(2)}, u32[]{:S(2)}) collective-permute-start(bf16[1,256,256]{2,1,0:T(8,128)(2,1)S(1)} %fusion.21), channel_id=1, source_target_pairs={{0,1},{1,0},{2,3},{3,2},{4,5},{5,4},{6,7},{7,6},{8,9},{9,8},{10,11... | collective-permute-start | bytes 393224 | tf_op jit(solution)/shard_map/ppermute | solution.py:18
  48.5 0.6 pad_clamp_fusion.1
  49.1 3.6 %collective-permute-done.22 = bf16[1,256,256]{2,1,0:T(8,128)(2,1)S(1)} collective-permute-done((bf16[1,256,256]{2,1,0:T(8,128)(2,1)S(1)}, bf16[1,256,256]{2,1,0:T(8,128)(2,1)S(1)}, u32[]{:S(2)}, u32[]{:S(2)}) %collective-permute-start.22) | collective-permute-done | bytes 131104 | tf_op jit(solution)/shard_map/ppermute | solution.py:18
  55.3 0.7 fusion.16
  56.1 1.5 %collective-permute-start.27 = (bf16[1,256,512]{2,1,0:T(8,128)(2,1)}, bf16[1,256,512]{2,1,0:T(8,128)(2,1)S(1)}, u32[]{:S(2)}, u32[]{:S(2)}) collective-permute-start(bf16[1,256,512]{2,1,0:T(8,128)(2,1)} %fusion.16), channel_id=1, source_target_pairs={{0,1},{1,0},{2,3},{3,2},{4,5},{5,4},{6,7},{7,6},{8,9},{9,8},{10,11... | collective-permute-start | bytes 786440 | tf_op jit(solution)/shard_map/ppermute | solution.py:18
  58.0 0.6 collective-permute-start
  58.9 8.2 %collective-permute-done = bf16[256,256]{1,0:T(8,128)(2,1)} collective-permute-done((bf16[256,256]{1,0:T(8,128)(2,1)S(1)}, bf16[256,256]{1,0:T(8,128)(2,1)}, u32[]{:S(2)}, u32[]{:S(2)}) %collective-permute-start) | collective-permute-done | bytes 131104 | tf_op jit(solution)/shard_map/ppermute | solution.py:18
  67.1 0.9 pad_maximum_fusion.1
  68.0 0.7 gather_fusion
  68.7 0.7 gather_fusion.1
  69.4 5.0 %multiply_reduce_fusion.2 = (f32[256]{0:T(256)S(1)}, f32[256,3584]{1,0:T(8,128)}) fusion(bf16[512,256]{1,0:T(8,128)(2,1)S(1)} %bitcast.121, bf16[512,3584]{1,0:T(8,128)(2,1)} %constant_dynamic-update-slice_fusion), kind=kOutput, calls=%fused_computation.7 | convolution fusion | flops 941358848 | bytes 7603200 | tf_op jit(solution)/shard_map/dot_general | solution.py:165
  74.4 1.5 %collective-permute-start.16 = (f32[256]{0:T(256)S(1)}, f32[256]{0:T(256)S(1)}, u32[]{:S(2)}, u32[]{:S(2)}) collective-permute-start(f32[256]{0:T(256)S(1)} %get-tuple-element.34), channel_id=1, source_target_pairs={{0,1},{1,0},{2,3},{3,2},{4,5},{5,4},{6,7},{7,6},{8,9},{9,8},{10,11... | collective-permute-start | bytes 3080 | tf_op jit(solution)/shard_map/ppermute | solution.py:18
  75.9 0.8 copy.122
  76.7 1.2 %collective-permute-done.16 = f32[256]{0:T(256)S(1)} collective-permute-done((f32[256]{0:T(256)S(1)}, f32[256]{0:T(256)S(1)}, u32[]{:S(2)}, u32[]{:S(2)}) %collective-permute-start.16) | collective-permute-done | bytes 1056 | tf_op jit(solution)/shard_map/ppermute | solution.py:18
  78.0 2.6 %multiply_reduce_fusion.1 = (f32[3584]{0:T(1024)S(1)}, f32[3584]{0:T(1024)S(1)}) fusion(f32[256,3584]{1,0:T(8,128)} %get-tuple-element.35, f32[256]{0:T(256)S(1)} %get-tuple-element.31), kind=kLoop, calls=%fused_computation.6 | loop fusion | flops 3662848 | bytes 3699712 | tf_op jit(solution)/shard_map/reduce_sum | solution.py:184
  80.7 1.0 bitcast_add_fusion.1
  82.0 0.6 collective-permute-start.18
  82.8 1.6 %collective-permute-start.24 = (bf16[4,36,256]{2,0,1:T(4,128)(2,1)S(1)}, bf16[4,36,256]{2,0,1:T(4,128)(2,1)S(1)}, u32[]{:S(2)}, u32[]{:S(2)}) collective-permute-start(bf16[4,36,256]{2,0,1:T(4,128)(2,1)S(1)} %bitcast.132), channel_id=1, source_target_pairs={{0,4},{2,6},{4,0},{6,2},{8,12},{10,14},{12,8},{14,10},{16,20},{18,... | collective-permute-start | bytes 221192 | tf_op jit(solution)/shard_map/ppermute | solution.py:18
  84.3 1.9 %collective-permute-done.18 = f32[2,3584]{1,0:T(2,128)S(1)} collective-permute-done((f32[2,3584]{1,0:T(2,128)S(1)}, f32[2,3584]{1,0:T(2,128)S(1)}, u32[]{:S(2)}, u32[]{:S(2)}) %collective-permute-start.18) | collective-permute-done | bytes 28704 | tf_op jit(solution)/shard_map/ppermute | solution.py:18
  86.3 0.5 collective-permute-start.19
  86.9 3.3 %collective-permute-done.19 = f32[2,3584]{1,0:T(2,128)S(1)} collective-permute-done((f32[2,3584]{1,0:T(2,128)S(1)}, f32[2,3584]{1,0:T(2,128)S(1)}, u32[]{:S(2)}, u32[]{:S(2)}) %collective-permute-start.19) | collective-permute-done | bytes 28704 | tf_op jit(solution)/shard_map/ppermute | solution.py:18
  90.2 1.3 %collective-permute-start.20 = (f32[2,3584]{1,0:T(2,128)S(1)}, f32[2,3584]{1,0:T(2,128)S(1)}, u32[]{:S(2)}, u32[]{:S(2)}) collective-permute-start(f32[2,3584]{1,0:T(2,128)S(1)} %add.141), channel_id=1, source_target_pairs={{0,16},{2,18},{4,20},{6,22},{8,24},{10,26},{12,28},{14,30},{16,0},... | collective-permute-start | bytes 86024 | tf_op jit(solution)/shard_map/ppermute | solution.py:18
  91.9 1.8 %collective-permute-start.25 = (bf16[2,36,256]{2,0,1:T(2,128)(2,1)S(1)}, bf16[2,36,256]{2,0,1:T(2,128)(2,1)S(1)}, u32[]{:S(2)}, u32[]{:S(2)}) collective-permute-start(bf16[2,36,256]{2,0,1:T(2,128)(2,1)S(1)} %bitcast.134), channel_id=1, source_target_pairs={{0,8},{2,10},{4,12},{6,14},{8,0},{10,2},{12,4},{14,6},{16,24},{18,... | collective-permute-start | bytes 110600 | tf_op jit(solution)/shard_map/ppermute | solution.py:18
  93.8 1.5 %collective-permute-done.20 = f32[2,3584]{1,0:T(2,128)S(1)} collective-permute-done((f32[2,3584]{1,0:T(2,128)S(1)}, f32[2,3584]{1,0:T(2,128)S(1)}, u32[]{:S(2)}, u32[]{:S(2)}) %collective-permute-start.20) | collective-permute-done | bytes 28704 | tf_op jit(solution)/shard_map/ppermute | solution.py:18
  95.4 0.6 divide_reduce_fusion
  96.0 1.5 %collective-permute-start.21 = (f32[]{:T(128)}, f32[]{:T(128)}, u32[]{:S(2)}, u32[]{:S(2)}) collective-permute-start(f32[]{:T(128)} %divide_reduce_fusion), channel_id=1, source_target_pairs={{0,1},{1,0},{2,3},{3,2},{4,5},{5,4},{6,7},{7,6},{8,9},{9,8},{10,11... | collective-permute-start | bytes 20 | tf_op jit(solution)/shard_map/ppermute | solution.py:18
  97.5 2.2 %collective-permute-done.21 = f32[]{:T(128)} collective-permute-done((f32[]{:T(128)}, f32[]{:T(128)}, u32[]{:S(2)}, u32[]{:S(2)}) %collective-permute-start.21) | collective-permute-done | bytes 36 | tf_op jit(solution)/shard_map/ppermute | solution.py:18
  101.0 4.4 %multiply_multiply_fusion = f32[256,3584]{1,0:T(8,128)} fusion(f32[256,3584]{1,0:T(8,128)} %get-tuple-element.35, f32[3584]{0:T(1024)S(1)} %rsqrt_multiply_fusion, f32[256]{0:T(256)S(1)} %get-tuple-element.30), kind=kLoop, calls=%fused_computation.5 | loop fusion | flops 1835008 | bytes 7355392 | tf_op jit(solution)/shard_map/mul | solution.py:191
  105.4 1.2 %collective-permute-start.26 = (bf16[1,36,256]{2,0,1:T(2,128)(2,1)S(1)}, bf16[1,36,256]{2,0,1:T(2,128)(2,1)S(1)}, u32[]{:S(2)}, u32[]{:S(2)}) collective-permute-start(bf16[1,36,256]{2,0,1:T(2,128)(2,1)S(1)} %dynamic-slice_convert_fusion.3), channel_id=1, source_target_pairs={{0,16},{2,18},{4,20},{6,22},{8,24},{10,26},{12,28},{14,30},{16,0},... | collective-permute-start | bytes 55304 | tf_op jit(solution)/shard_map/ppermute | solution.py:18
  106.6 0.9 fusion.15
  107.5 3.0 %collective-permute-done.26 = bf16[1,36,256]{2,0,1:T(2,128)(2,1)S(1)} collective-permute-done((bf16[1,36,256]{2,0,1:T(2,128)(2,1)S(1)}, bf16[1,36,256]{2,0,1:T(2,128)(2,1)S(1)}, u32[]{:S(2)}, u32[]{:S(2)}) %collective-permute-start.26) | collective-permute-done | bytes 18464 | tf_op jit(solution)/shard_map/ppermute | solution.py:18
  110.5 0.6 copy.162
  (95 shorter events, 6.8 us)
Async XLA Ops:
  0.6 10.0 %copy-start = (bf16[512,512]{1,0:T(8,128)(2,1)S(1)}, bf16[512,512]{1,0:T(8,128)(2,1)}, u32[]{:S(2)}) copy-start(bf16[512,512]{1,0:T(8,128)(2,1)} %param.16) | copy-start | bytes 1572868
  0.6 12.8 %copy-start.3 = (bf16[256,64]{0,1:T(8,128)(2,1)S(1)}, bf16[256,64]{0,1:T(8,128)(2,1)}, u32[]{:S(2)}) copy-start(bf16[256,64]{0,1:T(8,128)(2,1)} %param.15) | copy-start | bytes 98308
  0.7 18.5 %collective-permute-start.2 = (bf16[32,3584]{1,0:T(8,128)(2,1)}, bf16[32,3584]{1,0:T(8,128)(2,1)S(1)}, u32[]{:S(2)}, u32[]{:S(2)}) collective-permute-start(bf16[32,3584]{1,0:T(8,128)(2,1)} %param.9), channel_id=1, source_target_pairs={{0,4},{2,6},{4,0},{6,2},{8,12},{10,14},{12,8},{14,10},{16,20},{18,... | collective-permute-start | bytes 688136 | tf_op jit(solution)/shard_map/ppermute | solution.py:18
  3.7 15.8 %collective-permute-start.1 = (bf16[32,3584]{1,0:T(8,128)(2,1)}, bf16[32,3584]{1,0:T(8,128)(2,1)S(1)}, u32[]{:S(2)}, u32[]{:S(2)}) collective-permute-start(bf16[32,3584]{1,0:T(8,128)(2,1)} %param.9), channel_id=1, source_target_pairs={{0,2},{2,0},{4,6},{6,4},{8,10},{10,8},{12,14},{14,12},{16,18},{18,... | collective-permute-start | bytes 688136 | tf_op jit(solution)/shard_map/ppermute | solution.py:18
  3.7 13.0 %collective-permute-start.4 = (bf16[32,3584]{1,0:T(8,128)(2,1)}, bf16[32,3584]{1,0:T(8,128)(2,1)S(1)}, u32[]{:S(2)}, u32[]{:S(2)}) collective-permute-start(bf16[32,3584]{1,0:T(8,128)(2,1)} %param.9), channel_id=1, source_target_pairs={{0,8},{2,10},{4,12},{6,14},{8,0},{10,2},{12,4},{14,6},{16,24},{18,... | collective-permute-start | bytes 688136 | tf_op jit(solution)/shard_map/ppermute | solution.py:18
  5.3 13.8 %collective-permute-start.8 = (bf16[32,3584]{1,0:T(8,128)(2,1)}, bf16[32,3584]{1,0:T(8,128)(2,1)S(1)}, u32[]{:S(2)}, u32[]{:S(2)}) collective-permute-start(bf16[32,3584]{1,0:T(8,128)(2,1)} %param.9), channel_id=1, source_target_pairs={{0,16},{2,18},{4,20},{6,22},{8,24},{10,26},{12,28},{14,30},{16,0},... | collective-permute-start | bytes 688136 | tf_op jit(solution)/shard_map/ppermute | solution.py:18
  9.6 38.8 %copy-start.5 = (s32[1024]{0:T(1024)}, s32[1024]{0:T(1024)S(1)}, u32[]{:S(2)}) copy-start(s32[1024]{0:T(1024)S(1)} %pad_clamp_fusion) | copy-start | bytes 12292
  14.1 28.8 %copy-start.1 = (f32[256,3584]{1,0:T(8,128)S(1)}, f32[256,3584]{1,0:T(8,128)}, u32[]{:S(2)}) copy-start(f32[256,3584]{1,0:T(8,128)} %param.10) | copy-start | bytes 11010052
  16.7 11.8 %collective-permute-start.5 = (bf16[32,3584]{1,0:T(8,128)(2,1)S(1)}, bf16[32,3584]{1,0:T(8,128)(2,1)S(1)}, u32[]{:S(2)}, u32[]{:S(2)}) collective-permute-start(bf16[32,3584]{1,0:T(8,128)(2,1)S(1)} %collective-permute-done.4), channel_id=1, source_target_pairs={{0,2},{2,0},{4,6},{6,4},{8,10},{10,8},{12,14},{14,12},{16,18},{18,... | collective-permute-start | bytes 688136 | tf_op jit(solution)/shard_map/ppermute | solution.py:18
  16.7 12.3 %collective-permute-start.6 = (bf16[32,3584]{1,0:T(8,128)(2,1)S(1)}, bf16[32,3584]{1,0:T(8,128)(2,1)S(1)}, u32[]{:S(2)}, u32[]{:S(2)}) collective-permute-start(bf16[32,3584]{1,0:T(8,128)(2,1)S(1)} %collective-permute-done.4), channel_id=1, source_target_pairs={{0,4},{2,6},{4,0},{6,2},{8,12},{10,14},{12,8},{14,10},{16,20},{18,... | collective-permute-start | bytes 688136 | tf_op jit(solution)/shard_map/ppermute | solution.py:18
  19.1 18.9 %collective-permute-start.9 = (bf16[32,3584]{1,0:T(8,128)(2,1)S(1)}, bf16[32,3584]{1,0:T(8,128)(2,1)S(1)}, u32[]{:S(2)}, u32[]{:S(2)}) collective-permute-start(bf16[32,3584]{1,0:T(8,128)(2,1)S(1)} %collective-permute-done.8), channel_id=1, source_target_pairs={{0,2},{2,0},{4,6},{6,4},{8,10},{10,8},{12,14},{14,12},{16,18},{18,... | collective-permute-start | bytes 688136 | tf_op jit(solution)/shard_map/ppermute | solution.py:18
  19.1 8.0 %collective-permute-start.12 = (bf16[32,3584]{1,0:T(8,128)(2,1)S(1)}, bf16[32,3584]{1,0:T(8,128)(2,1)S(1)}, u32[]{:S(2)}, u32[]{:S(2)}) collective-permute-start(bf16[32,3584]{1,0:T(8,128)(2,1)S(1)} %collective-permute-done.8), channel_id=1, source_target_pairs={{0,8},{2,10},{4,12},{6,14},{8,0},{10,2},{12,4},{14,6},{16,24},{18,... | collective-permute-start | bytes 688136 | tf_op jit(solution)/shard_map/ppermute | solution.py:18
  19.6 1.6 %collective-permute-start.3 = (bf16[32,3584]{1,0:T(8,128)(2,1)S(1)}, bf16[32,3584]{1,0:T(8,128)(2,1)S(1)}, u32[]{:S(2)}, u32[]{:S(2)}) collective-permute-start(bf16[32,3584]{1,0:T(8,128)(2,1)S(1)} %collective-permute-done.2), channel_id=1, source_target_pairs={{0,2},{2,0},{4,6},{6,4},{8,10},{10,8},{12,14},{14,12},{16,18},{18,... | collective-permute-start | bytes 688136 | tf_op jit(solution)/shard_map/ppermute | solution.py:18
  21.2 8.5 %collective-permute-start.10 = (bf16[32,3584]{1,0:T(8,128)(2,1)S(1)}, bf16[32,3584]{1,0:T(8,128)(2,1)S(1)}, u32[]{:S(2)}, u32[]{:S(2)}) collective-permute-start(bf16[32,3584]{1,0:T(8,128)(2,1)S(1)} %collective-permute-done.8), channel_id=1, source_target_pairs={{0,4},{2,6},{4,0},{6,2},{8,12},{10,14},{12,8},{14,10},{16,20},{18,... | collective-permute-start | bytes 688136 | tf_op jit(solution)/shard_map/ppermute | solution.py:18
  27.1 13.7 %collective-permute-start.13 = (bf16[32,3584]{1,0:T(8,128)(2,1)S(1)}, bf16[32,3584]{1,0:T(8,128)(2,1)S(1)}, u32[]{:S(2)}, u32[]{:S(2)}) collective-permute-start(bf16[32,3584]{1,0:T(8,128)(2,1)S(1)} %collective-permute-done.12), channel_id=1, source_target_pairs={{0,2},{2,0},{4,6},{6,4},{8,10},{10,8},{12,14},{14,12},{16,18},{18,... | collective-permute-start | bytes 688136 | tf_op jit(solution)/shard_map/ppermute | solution.py:18
  28.6 8.0 %collective-permute-start.14 = (bf16[32,3584]{1,0:T(8,128)(2,1)S(1)}, bf16[32,3584]{1,0:T(8,128)(2,1)S(1)}, u32[]{:S(2)}, u32[]{:S(2)}) collective-permute-start(bf16[32,3584]{1,0:T(8,128)(2,1)S(1)} %collective-permute-done.12), channel_id=1, source_target_pairs={{0,4},{2,6},{4,0},{6,2},{8,12},{10,14},{12,8},{14,10},{16,20},{18,... | collective-permute-start | bytes 688136 | tf_op jit(solution)/shard_map/ppermute | solution.py:18
  29.1 7.5 %collective-permute-start.7 = (bf16[32,3584]{1,0:T(8,128)(2,1)S(1)}, bf16[32,3584]{1,0:T(8,128)(2,1)S(1)}, u32[]{:S(2)}, u32[]{:S(2)}) collective-permute-start(bf16[32,3584]{1,0:T(8,128)(2,1)S(1)} %collective-permute-done.6), channel_id=1, source_target_pairs={{0,2},{2,0},{4,6},{6,4},{8,10},{10,8},{12,14},{14,12},{16,18},{18,... | collective-permute-start | bytes 688136 | tf_op jit(solution)/shard_map/ppermute | solution.py:18
  29.7 9.7 %collective-permute-start.11 = (bf16[32,3584]{1,0:T(8,128)(2,1)S(1)}, bf16[32,3584]{1,0:T(8,128)(2,1)S(1)}, u32[]{:S(2)}, u32[]{:S(2)}) collective-permute-start(bf16[32,3584]{1,0:T(8,128)(2,1)S(1)} %collective-permute-done.10), channel_id=1, source_target_pairs={{0,2},{2,0},{4,6},{6,4},{8,10},{10,8},{12,14},{14,12},{16,18},{18,... | collective-permute-start | bytes 688136 | tf_op jit(solution)/shard_map/ppermute | solution.py:18
  36.6 5.6 %collective-permute-start.15 = (bf16[32,3584]{1,0:T(8,128)(2,1)S(1)}, bf16[32,3584]{1,0:T(8,128)(2,1)S(1)}, u32[]{:S(2)}, u32[]{:S(2)}) collective-permute-start(bf16[32,3584]{1,0:T(8,128)(2,1)S(1)} %collective-permute-done.14), channel_id=1, source_target_pairs={{0,2},{2,0},{4,6},{6,4},{8,10},{10,8},{12,14},{14,12},{16,18},{18,... | collective-permute-start | bytes 688136 | tf_op jit(solution)/shard_map/ppermute | solution.py:18
  46.7 6.0 %collective-permute-start.22 = (bf16[1,256,256]{2,1,0:T(8,128)(2,1)S(1)}, bf16[1,256,256]{2,1,0:T(8,128)(2,1)S(1)}, u32[]{:S(2)}, u32[]{:S(2)}) collective-permute-start(bf16[1,256,256]{2,1,0:T(8,128)(2,1)S(1)} %fusion.21), channel_id=1, source_target_pairs={{0,1},{1,0},{2,3},{3,2},{4,5},{5,4},{6,7},{7,6},{8,9},{9,8},{10,11... | collective-permute-start | bytes 393224 | tf_op jit(solution)/shard_map/ppermute | solution.py:18
  52.9 1.1 %copy-start.2 = (bf16[256,512]{1,0:T(8,128)(2,1)S(1)}, bf16[256,512]{1,0:T(8,128)(2,1)}, u32[]{:S(2)}) copy-start(bf16[256,512]{1,0:T(8,128)(2,1)} %param.14) | copy-start | bytes 786436
  56.1 50.5 %collective-permute-start.27 = (bf16[1,256,512]{2,1,0:T(8,128)(2,1)}, bf16[1,256,512]{2,1,0:T(8,128)(2,1)S(1)}, u32[]{:S(2)}, u32[]{:S(2)}) collective-permute-start(bf16[1,256,512]{2,1,0:T(8,128)(2,1)} %fusion.16), channel_id=1, source_target_pairs={{0,1},{1,0},{2,3},{3,2},{4,5},{5,4},{6,7},{7,6},{8,9},{9,8},{10,11... | collective-permute-start | bytes 786440 | tf_op jit(solution)/shard_map/ppermute | solution.py:18
  58.0 9.0 %collective-permute-start = (bf16[256,256]{1,0:T(8,128)(2,1)S(1)}, bf16[256,256]{1,0:T(8,128)(2,1)}, u32[]{:S(2)}, u32[]{:S(2)}) collective-permute-start(bf16[256,256]{1,0:T(8,128)(2,1)S(1)} %copy.104), channel_id=1, source_target_pairs={{0,1},{1,0},{2,3},{3,2},{4,5},{5,4},{6,7},{7,6},{8,9},{9,8},{10,11... | collective-permute-start | bytes 393224 | tf_op jit(solution)/shard_map/ppermute | solution.py:18
  58.7 22.1 %collective-permute-start.23 = (bf16[8,36,256]{2,0,1:T(8,128)(2,1)S(1)}, bf16[8,36,256]{2,0,1:T(8,128)(2,1)}, u32[]{:S(2)}, u32[]{:S(2)}) collective-permute-start(bf16[8,36,256]{2,0,1:T(8,128)(2,1)S(1)} %bitcast.128), channel_id=1, source_target_pairs={{0,2},{2,0},{4,6},{6,4},{8,10},{10,8},{12,14},{14,12},{16,18},{18,... | collective-permute-start | bytes 442376 | tf_op jit(solution)/shard_map/ppermute | solution.py:18
  69.4 8.6 %copy-start.6 = (f32[256]{0:T(256)S(1)}, f32[256]{0:T(256)}, u32[]{:S(2)}) copy-start(f32[256]{0:T(256)} %param.11) | copy-start | bytes 3076
  74.4 3.6 %collective-permute-start.16 = (f32[256]{0:T(256)S(1)}, f32[256]{0:T(256)S(1)}, u32[]{:S(2)}, u32[]{:S(2)}) collective-permute-start(f32[256]{0:T(256)S(1)} %get-tuple-element.34), channel_id=1, source_target_pairs={{0,1},{1,0},{2,3},{3,2},{4,5},{5,4},{6,7},{7,6},{8,9},{9,8},{10,11... | collective-permute-start | bytes 3080 | tf_op jit(solution)/shard_map/ppermute | solution.py:18
  78.0 17.4 %copy-start.4 = (f32[3584]{0:T(1024)S(1)}, f32[3584]{0:T(1024)}, u32[]{:S(2)}) copy-start(f32[3584]{0:T(1024)} %param.12) | copy-start | bytes 43012
  80.7 1.3 %collective-permute-start.17 = (f32[2,3584]{1,0:T(2,128)S(1)}, f32[2,3584]{1,0:T(2,128)S(1)}, u32[]{:S(2)}, u32[]{:S(2)}) collective-permute-start(f32[2,3584]{1,0:T(2,128)S(1)} %pad_maximum_fusion.4), channel_id=1, source_target_pairs={{0,2},{2,0},{4,6},{6,4},{8,10},{10,8},{12,14},{14,12},{16,18},{18,... | collective-permute-start | bytes 86024 | tf_op jit(solution)/shard_map/ppermute | solution.py:18
  82.0 4.2 %collective-permute-start.18 = (f32[2,3584]{1,0:T(2,128)S(1)}, f32[2,3584]{1,0:T(2,128)S(1)}, u32[]{:S(2)}, u32[]{:S(2)}) collective-permute-start(f32[2,3584]{1,0:T(2,128)S(1)} %fusion.35), channel_id=1, source_target_pairs={{0,4},{2,6},{4,0},{6,2},{8,12},{10,14},{12,8},{14,10},{16,20},{18,... | collective-permute-start | bytes 86024 | tf_op jit(solution)/shard_map/ppermute | solution.py:18
  82.8 8.8 %collective-permute-start.24 = (bf16[4,36,256]{2,0,1:T(4,128)(2,1)S(1)}, bf16[4,36,256]{2,0,1:T(4,128)(2,1)S(1)}, u32[]{:S(2)}, u32[]{:S(2)}) collective-permute-start(bf16[4,36,256]{2,0,1:T(4,128)(2,1)S(1)} %bitcast.132), channel_id=1, source_target_pairs={{0,4},{2,6},{4,0},{6,2},{8,12},{10,14},{12,8},{14,10},{16,20},{18,... | collective-permute-start | bytes 221192 | tf_op jit(solution)/shard_map/ppermute | solution.py:18
  86.3 3.9 %collective-permute-start.19 = (f32[2,3584]{1,0:T(2,128)S(1)}, f32[2,3584]{1,0:T(2,128)S(1)}, u32[]{:S(2)}, u32[]{:S(2)}) collective-permute-start(f32[2,3584]{1,0:T(2,128)S(1)} %fusion.61), channel_id=1, source_target_pairs={{0,8},{2,10},{4,12},{6,14},{8,0},{10,2},{12,4},{14,6},{16,24},{18,... | collective-permute-start | bytes 86024 | tf_op jit(solution)/shard_map/ppermute | solution.py:18
  90.2 5.0 %collective-permute-start.20 = (f32[2,3584]{1,0:T(2,128)S(1)}, f32[2,3584]{1,0:T(2,128)S(1)}, u32[]{:S(2)}, u32[]{:S(2)}) collective-permute-start(f32[2,3584]{1,0:T(2,128)S(1)} %add.141), channel_id=1, source_target_pairs={{0,16},{2,18},{4,20},{6,22},{8,24},{10,26},{12,28},{14,30},{16,0},... | collective-permute-start | bytes 86024 | tf_op jit(solution)/shard_map/ppermute | solution.py:18
  91.9 13.5 %collective-permute-start.25 = (bf16[2,36,256]{2,0,1:T(2,128)(2,1)S(1)}, bf16[2,36,256]{2,0,1:T(2,128)(2,1)S(1)}, u32[]{:S(2)}, u32[]{:S(2)}) collective-permute-start(bf16[2,36,256]{2,0,1:T(2,128)(2,1)S(1)} %bitcast.134), channel_id=1, source_target_pairs={{0,8},{2,10},{4,12},{6,14},{8,0},{10,2},{12,4},{14,6},{16,24},{18,... | collective-permute-start | bytes 110600 | tf_op jit(solution)/shard_map/ppermute | solution.py:18
  96.0 3.7 %collective-permute-start.21 = (f32[]{:T(128)}, f32[]{:T(128)}, u32[]{:S(2)}, u32[]{:S(2)}) collective-permute-start(f32[]{:T(128)} %divide_reduce_fusion), channel_id=1, source_target_pairs={{0,1},{1,0},{2,3},{3,2},{4,5},{5,4},{6,7},{7,6},{8,9},{9,8},{10,11... | collective-permute-start | bytes 20 | tf_op jit(solution)/shard_map/ppermute | solution.py:18
  105.4 5.0 %collective-permute-start.26 = (bf16[1,36,256]{2,0,1:T(2,128)(2,1)S(1)}, bf16[1,36,256]{2,0,1:T(2,128)(2,1)S(1)}, u32[]{:S(2)}, u32[]{:S(2)}) collective-permute-start(bf16[1,36,256]{2,0,1:T(2,128)(2,1)S(1)} %dynamic-slice_convert_fusion.3), channel_id=1, source_target_pairs={{0,16},{2,18},{4,20},{6,22},{8,24},{10,26},{12,28},{14,30},{16,0},... | collective-permute-start | bytes 55304 | tf_op jit(solution)/shard_map/ppermute | solution.py:18
